TPU v7x, 256 devices: a whole 4x4x8 slice. The times are simulated.
256 devices in a mesh: rows: 32 (over y, z), cols: 8 (over x, core).
Axes of the slice: x: 4, y: 4, z: 8, core: 2. Of those that a mesh axis runs over, the one named last changes fastest.
Arguments:
- snapshots: bfloat16 [524288, 2048], P(('rows', 'cols')), may hold values from -24 to 24
- test_matrix: bfloat16 [2048, 256], replicated, may hold values from -0.125 to 0.125
Outputs:
- basis: float32 [524288, 256], P(('rows', 'cols'))
- coeffs: float32 [256, 2048], P('rows', 'cols')
All inputs are finite; a program needn't handle non-finite values.
Results may differ from a plain program's by a relative error of at most 0.0005.
Values sent between devices are 32-bit elements; how exact they have to be, the bound alone decides.
A program may use at most 64 MiB of HBM per device.

v0:
```python
import math
import jax
import jax.numpy as jnp
from jax import lax
from jax.sharding import PartitionSpec as P


def cross_product(left, right):
    return lax.dot_general(
        left,
        right,
        (((0,), (0,)), ((), ())),
        precision=lax.Precision.HIGHEST,
        preferred_element_type=jnp.float32,
    )


def lower_inverse(gram):
    lower = jnp.linalg.cholesky(gram)
    identity = jnp.eye(gram.shape[0], dtype=gram.dtype)
    return jax.scipy.linalg.solve_triangular(lower, identity, lower=True)


def body(snapshots, test_matrix):
    n_rows = lax.axis_size("rows")
    n_cols = lax.axis_size("cols")
    rows_here = snapshots.shape[0]
    total_rows = rows_here * n_rows * n_cols
    sketch = jnp.dot(snapshots, test_matrix, preferred_element_type=jnp.float32)
    gram_local = cross_product(sketch, sketch)
    summed = lax.psum(gram_local, ("rows", "cols"))
    inverse_low = lower_inverse(summed)
    basis_full = lax.dot_general(
        sketch,
        inverse_low,
        (((1,), (1,)), ((), ())),
        precision=lax.Precision.HIGHEST,
        preferred_element_type=jnp.float32,
    ) * math.sqrt(total_rows)
    basis_half = basis_full.astype(jnp.bfloat16)
    grid_part = lax.psum_scatter(
        lax.dot_general(
            snapshots, basis_half, (((0,), (0,)), ((), ())), preferred_element_type=jnp.float32
        ),
        "cols",
        scatter_dimension=0,
        tiled=True,
    )
    projected = lax.psum_scatter(grid_part.T, "rows", scatter_dimension=0, tiled=True)
    coeffs = projected * (1.0 / math.sqrt(total_rows))
    return (basis_full, coeffs)


def solution(mesh):
    placed = (P(("rows", "cols"), None), P())
    return jax.shard_map(
        body,
        mesh=mesh,
        in_specs=placed,
        out_specs=(P(("rows", "cols"), None), P("rows", "cols")),
        check_vma=False,
    )
```

profile of v0, /device:TPU:2, one launch (start us, length us, event | category | flops | bytes accessed | tf_op | source)
XLA Modules:
  0.0 614.2 jit_solution(18201936936618423826)
XLA Ops:
  7.2 0.0 copy-start
  7.2 0.0 all-reduce.3.cloned.1.call-start
  7.2 1.2 copy-done
  8.4 5.7 fusion.14
  14.1 4.2 fusion.15
  18.3 0.0 all-reduce.3.cloned.1.call-update
  18.3 0.2 reduce-scatter.3.cloned.1.call-start
  18.6 253.1 %all-reduce.3.cloned.1.call-done = f32[256,256]{0,1:T(8,128)} async-done(((f32[256,256]{0,1:T(8,128)}), f32[256,256]{0,1:T(8,128)}) %all-reduce.3.cloned.1.call-update) | async-done | bytes 262160 | tf_op jit(solution)/shard_map/psum | solution.py:31
  271.7 1.1 copy.5
  272.8 1.0 fusion.4
  273.7 0.0 copy-start.3
  273.8 0.7 copy-done.3
  274.5 11.7 %cholesky.50 = f32[128,128]{1,0:T(8,128)S(1)} custom-call(f32[128,128]{1,0:T(8,128)S(1)} %cholesky.118), custom_call_target="Cholesky" | custom-call | tf_op jit(solution)/shard_map/jit(cholesky)/cholesky | solution.py:19
  286.2 10.4 %custom-call.15 = f32[1,128,128]{1,2,0:T(8,128)} custom-call(f32[1,128,128]{2,1,0:T(8,128)S(1)} %get-tuple-element.23), custom_call_target="InvertDiagBlocksLowerTriangular" | custom-call | tf_op jit(solution)/shard_map/jit(cholesky)/cholesky | solution.py:19
  296.7 1.1 constant_dynamic-update-slice_fusion.1
  297.7 1.7 convolution_subtract_fusion.1
  299.5 12.5 %cholesky.105 = f32[128,128]{1,0:T(8,128)S(1)} custom-call(f32[128,128]{1,0:T(8,128)} %convolution_subtract_fusion.1), custom_call_target="Cholesky" | custom-call | tf_op jit(solution)/shard_map/jit(cholesky)/cholesky | solution.py:19
  312.1 0.0 copy-start.2
  312.1 0.7 compare_reduce_fusion
  314.0 0.0 copy-done.2
  314.1 1.0 select_select_fusion
  315.0 0.1 triangular_solve.63
  315.1 5.5 while.1
  315.3 0.6 fusion.27
  315.9 2.0 bitcast_dynamic-update-slice_fusion.2
  317.9 0.6 fusion.27
  318.5 2.1 bitcast_dynamic-update-slice_fusion.2
  320.6 21.1 %custom-call.16 = f32[2,128,128]{1,2,0:T(8,128)} custom-call(f32[2,128,128]{2,1,0:T(8,128)} %get-tuple-element.9), custom_call_target="InvertDiagBlocksLowerTriangular" | custom-call | tf_op jit(solution)/shard_map/jit(_solve_triangular)/triangular_solve | solution.py:21
  341.7 1.1 fusion.5
  342.8 0.3 convolution_subtract_fusion
  343.1 1.2 fusion.8
  344.3 1.9 convolution_multiply_fusion
  346.2 0.0 copy-start.1
  346.2 1.3 copy-done.1
  347.5 7.1 %convolution_bitcast_fusion = f32[2048,256]{0,1:T(8,128)} fusion(bf16[2048,2048]{1,0:T(8,128)(2,1)} %param.2, f32[2048,256]{1,0:T(8,128)S(1)} %convolution_multiply_fusion), kind=kOutput, calls=%fused_computation.2 | convolution fusion | flops 2148007936 | bytes 12582912 | tf_op jit(solution)/shard_map/dot_general | solution.py:42
  354.7 0.0 reduce-scatter.3.cloned.1.call-update
  354.7 0.0 reduce-scatter.5.cloned.1.call-start
  354.7 31.7 %reduce-scatter.3.cloned.1.call-done = f32[256,256]{0,1:T(8,128)} async-done(((f32[2048,256]{0,1:T(8,128)}), f32[256,256]{0,1:T(8,128)}) %reduce-scatter.3.cloned.1.call-update) | async-done | bytes 262160 | tf_op jit(solution)/shard_map/reduce_scatter | solution.py:41
  386.5 0.0 reduce-scatter.5.cloned.1.call-update
  386.5 219.9 %reduce-scatter.5.cloned.1.call-done = f32[8,256]{1,0:T(8,128)} async-done(((f32[256,256]{1,0:T(8,128)}), f32[8,256]{1,0:T(8,128)}) %reduce-scatter.5.cloned.1.call-update) | async-done | bytes 8208 | tf_op jit(solution)/shard_map/reduce_scatter | solution.py:49
  606.4 1.3 broadcast_multiply_fusion
  (9 shorter events, 0.1 us)
Async XLA Ops:
  7.2 1.2 copy-start
  7.2 264.5 %all-reduce.3.cloned.1.call-start = ((), (), s32[]{:S(2)}) async-start(), calls=%async_computation.2 | async-start | bytes 524288 | tf_op jit(solution)/shard_map/psum | solution.py:31
  18.3 368.2 %reduce-scatter.3.cloned.1.call-start = ((), (), s32[]{:S(2)}) async-start(), calls=%async_computation.3 | async-start | bytes 2359296 | tf_op jit(solution)/shard_map/reduce_scatter | solution.py:41
  273.7 0.7 copy-start.3
  312.1 2.0 copy-start.2
  346.2 1.3 copy-start.1
  354.7 251.7 %reduce-scatter.5.cloned.1.call-start = ((), (), s32[]{:S(2)}) async-start(), calls=%async_computation.4 | async-start | bytes 270336 | tf_op jit(solution)/shard_map/reduce_scatter | solution.py:49
Sparse Core Ops, SparseCore 0:
  18.4 253.1 all-reduce.2
  354.8 31.6 reduce-scatter.2
  390.3 216.0 reduce-scatter.4
where the time goes:
time: 615 us; the launch traced here: 614 us
  waiting for transfers between devices  505 us (82%)
  other arithmetic  59.9 us (10%)
  matrix products  24.3 us (4%)
  between operations  15.1 us (2%)
  local copies, waits for them, and re-layouts  9.67 us (2%)
    psum x1, waiting for transfers between devices, body(): summed = lax.psum(gram_local, ('rows', 'cols'))  253 us
    reduce_scatter x1, waiting for transfers between devices, body(): lax.psum_scatter(grid_part.T, 'rows', scatter_dimension=0, tiled=True)  220 us
    another operation x6, other arithmetic, lower_inverse(): lower = jnp.linalg.cholesky(gram)  35.5 us
    reduce_scatter x1, waiting for transfers between devices, body(): lax.psum_scatter(lax.dot_general(snapshots, basis_half, (((0,), (0,)), ((...  31.7 us
    another operation x3, other arithmetic, lower_inverse(): return jax.scipy.linalg.solve_triangular(lower, identity, lower=True)  22.1 us
  transfers between devices with their start and end apart: 3, of which 3 were waited for; matrix products, arithmetic and copies ran while one was open for 0% of the time, Pallas kernels for 0%

commit v1 on v0

--- a/solution.py
+++ b/solution.py
@@ -28,7 +28,7 @@
     total_rows = rows_here * n_rows * n_cols
     sketch = jnp.dot(snapshots, test_matrix, preferred_element_type=jnp.float32)
     gram_local = cross_product(sketch, sketch)
-    summed = lax.psum(gram_local, ("rows", "cols"))
+    summed = lax.psum(lax.psum(gram_local, "rows"), "cols")
     inverse_low = lower_inverse(summed)
     basis_full = lax.dot_general(
         sketch,

time: 615 us -> 573 us (0.932)
  waiting for transfers between devices: 505 us -> 463 us
    psum x1 -> x2, waiting for transfers between devices: 253 us -> 209 us  [body(): summed = lax.psum(lax.psum(gram_local, 'rows'), 'cols')]
  transfers between devices with their start and end apart: 3 -> 4, of which waited for: 3 -> 4; matrix products, arithmetic and copies ran while one was open for 0% -> 0% of each run, Pallas kernels for 0% -> 0%
where the time goes in v1:
time: 573 us
  waiting for transfers between devices  463 us (81%)
  other arithmetic  59.9 us (10%)
  matrix products  24.3 us (4%)
  between operations  15.2 us (3%)
  local copies, waits for them, and re-layouts  9.66 us (2%)
    reduce_scatter x1, waiting for transfers between devices, body(): lax.psum_scatter(grid_part.T, 'rows', scatter_dimension=0, tiled=True)  220 us
    psum x2, waiting for transfers between devices, body(): summed = lax.psum(lax.psum(gram_local, 'rows'), 'cols')  209 us
    another operation x6, other arithmetic, lower_inverse(): lower = jnp.linalg.cholesky(gram)  35.5 us
    reduce_scatter x1, waiting for transfers between devices, body(): lax.psum_scatter(lax.dot_general(snapshots, basis_half, (((0,), (0,)), ((...  34.3 us
    another operation x3, other arithmetic, lower_inverse(): return jax.scipy.linalg.solve_triangular(lower, identity, lower=True)  22.1 us
  transfers between devices with their start and end apart: 4, of which 4 were waited for; matrix products, arithmetic and copies ran while one was open for 0% of the time, Pallas kernels for 0%

profile of v1, /device:TPU:2, one launch (start us, length us, event | category | flops | bytes accessed | tf_op | source)
XLA Modules:
  0.0 572.8 jit_solution(7811774445470731395)
XLA Ops:
  7.2 0.0 copy-start
  7.2 0.0 all-reduce.4.cloned.1.call-start
  7.2 1.2 copy-done
  8.4 5.7 %fusion.14 = f32[2048,256]{1,0:T(8,128)S(1)} fusion(bf16[2048,2048]{1,0:T(8,128)(2,1)} %param.2, bf16[2048,256]{1,0:T(8,128)(2,1)S(1)} %copy-done), kind=kOutput, calls=%fused_computation.37 | convolution fusion | flops 2147483648 | bytes 11534336 | tf_op jit(solution)/shard_map/dot_general | solution.py:29
  14.1 4.2 fusion.15
  18.3 0.0 all-reduce.4.cloned.1.call-update
  18.3 0.0 all-reduce.6.cloned.1.call-start
  18.4 147.3 %all-reduce.4.cloned.1.call-done = f32[256,256]{0,1:T(8,128)} async-done(((f32[256,256]{0,1:T(8,128)}), f32[256,256]{0,1:T(8,128)}) %all-reduce.4.cloned.1.call-update) | async-done | bytes 262160 | tf_op jit(solution)/shard_map/psum | solution.py:31
  165.6 0.0 all-reduce.6.cloned.1.call-update
  165.7 0.2 reduce-scatter.3.cloned.1.call-start
  165.9 61.7 %all-reduce.6.cloned.1.call-done = f32[256,256]{0,1:T(8,128)} async-done(((f32[256,256]{0,1:T(8,128)}), f32[256,256]{0,1:T(8,128)}) %all-reduce.6.cloned.1.call-update) | async-done | bytes 262160 | tf_op jit(solution)/shard_map/psum | solution.py:31
  227.7 1.1 copy.5
  228.8 1.0 fusion.4
  229.7 0.0 copy-start.3
  229.8 0.7 copy-done.3
  230.5 11.7 %cholesky.50 = f32[128,128]{1,0:T(8,128)S(1)} custom-call(f32[128,128]{1,0:T(8,128)S(1)} %cholesky.118), custom_call_target="Cholesky" | custom-call | tf_op jit(solution)/shard_map/jit(cholesky)/cholesky | solution.py:19
  242.2 10.4 %custom-call.15 = f32[1,128,128]{1,2,0:T(8,128)} custom-call(f32[1,128,128]{2,1,0:T(8,128)S(1)} %get-tuple-element.23), custom_call_target="InvertDiagBlocksLowerTriangular" | custom-call | tf_op jit(solution)/shard_map/jit(cholesky)/cholesky | solution.py:19
  252.7 1.1 constant_dynamic-update-slice_fusion.1
  253.7 1.7 convolution_subtract_fusion.1
  255.5 12.5 %cholesky.105 = f32[128,128]{1,0:T(8,128)S(1)} custom-call(f32[128,128]{1,0:T(8,128)} %convolution_subtract_fusion.1), custom_call_target="Cholesky" | custom-call | tf_op jit(solution)/shard_map/jit(cholesky)/cholesky | solution.py:19
  268.1 0.0 copy-start.2
  268.1 0.7 compare_reduce_fusion
  270.0 0.0 copy-done.2
  270.1 1.0 select_select_fusion
  271.0 0.1 triangular_solve.63
  271.1 5.5 while.1
  271.3 0.6 fusion.27
  271.9 2.1 bitcast_dynamic-update-slice_fusion.2
  274.0 0.6 fusion.27
  274.5 2.0 bitcast_dynamic-update-slice_fusion.2
  276.6 21.1 %custom-call.16 = f32[2,128,128]{1,2,0:T(8,128)} custom-call(f32[2,128,128]{2,1,0:T(8,128)} %get-tuple-element.9), custom_call_target="InvertDiagBlocksLowerTriangular" | custom-call | tf_op jit(solution)/shard_map/jit(_solve_triangular)/triangular_solve | solution.py:21
  297.7 1.1 fusion.5
  298.8 0.3 convolution_subtract_fusion
  299.1 1.2 fusion.8
  300.2 1.9 convolution_multiply_fusion
  302.2 0.0 copy-start.1
  302.2 1.3 copy-done.1
  303.5 7.1 %convolution_bitcast_fusion = f32[2048,256]{0,1:T(8,128)} fusion(bf16[2048,2048]{1,0:T(8,128)(2,1)} %param.2, f32[2048,256]{1,0:T(8,128)S(1)} %convolution_multiply_fusion), kind=kOutput, calls=%fused_computation.2 | convolution fusion | flops 2148007936 | bytes 12582912 | tf_op jit(solution)/shard_map/dot_general | solution.py:42
  310.6 0.0 reduce-scatter.3.cloned.1.call-update
  310.7 0.0 reduce-scatter.5.cloned.1.call-start
  310.7 34.3 %reduce-scatter.3.cloned.1.call-done = f32[256,256]{0,1:T(8,128)} async-done(((f32[2048,256]{0,1:T(8,128)}), f32[256,256]{0,1:T(8,128)}) %reduce-scatter.3.cloned.1.call-update) | async-done | bytes 262160 | tf_op jit(solution)/shard_map/reduce_scatter | solution.py:41
  345.1 0.0 reduce-scatter.5.cloned.1.call-update
  345.1 219.9 %reduce-scatter.5.cloned.1.call-done = f32[8,256]{1,0:T(8,128)} async-done(((f32[256,256]{1,0:T(8,128)}), f32[8,256]{1,0:T(8,128)}) %reduce-scatter.5.cloned.1.call-update) | async-done | bytes 8208 | tf_op jit(solution)/shard_map/reduce_scatter | solution.py:49
  565.0 1.3 broadcast_multiply_fusion
  (9 shorter events, 0.1 us)
Async XLA Ops:
  7.2 1.2 copy-start
  7.2 158.4 %all-reduce.4.cloned.1.call-start = ((), (), s32[]{:S(2)}) async-start(), calls=%async_computation.2 | async-start | bytes 524288 | tf_op jit(solution)/shard_map/psum | solution.py:31
  18.3 209.4 %all-reduce.6.cloned.1.call-start = ((), (), s32[]{:S(2)}) async-start(), calls=%async_computation.3 | async-start | bytes 524288 | tf_op jit(solution)/shard_map/psum | solution.py:31
  165.7 179.4 %reduce-scatter.3.cloned.1.call-start = ((), (), s32[]{:S(2)}) async-start(), calls=%async_computation.4 | async-start | bytes 2359296 | tf_op jit(solution)/shard_map/reduce_scatter | solution.py:41
  229.7 0.7 copy-start.3
  268.1 2.0 copy-start.2
  302.2 1.3 copy-start.1
  310.7 254.3 %reduce-scatter.5.cloned.1.call-start = ((), (), s32[]{:S(2)}) async-start(), calls=%async_computation.5 | async-start | bytes 270336 | tf_op jit(solution)/shard_map/reduce_scatter | solution.py:49
Sparse Core Ops, SparseCore 0:
  18.4 147.1 all-reduce.3
  167.9 59.6 all-reduce.5
  310.8 34.2 reduce-scatter.2
  349.2 215.7 reduce-scatter.4
